TPU v7x, 256 devices: a whole 4x4x8 slice. The times are simulated.
256 devices in a mesh: section: 8 (over z), dp: 32 (over x, y, core).
Axes of the slice: x: 4, y: 4, z: 8, core: 2. Of those that a mesh axis runs over, the one named last changes fastest.
Arguments:
- inputs: bfloat16 [8192, 2048], P('dp'), may hold values from -6 to 6
- order: int32 [32, 2], P('dp'), may hold values from 0 to 1, each once within a row
- image_start: int32 [32, 2], P('dp'), may hold values from 0 to 112, as said below
- image_len: int32 [32, 2], P('dp'), may hold values from 16 to 64
- norm_gain: float32 [8, 2048], P('section'), may hold values from 0.25 to 1.75
- qkv_weight: bfloat16 [8, 2048, 6144], P('section', 'dp'), may hold values from -0.125 to 0.125
- q_gain: float32 [8, 2048], P('section'), may hold values from 0.5 to 2.5
- k_gain: float32 [8, 2048], P('section'), may hold values from 0.5 to 2.5
- o_weight: bfloat16 [8, 2048, 2048], P('section'), may hold values from -0.125 to 0.125
Outputs:
- section_outputs: bfloat16 [8, 8192, 2048], P('section', 'dp')
Inputs may be any that keep to these rules, and one draw needn't show every extreme that they name: `order`: each row is a permutation of the micro-batch numbers. image_start + image_len <= 128 for every micro-batch.
All inputs are finite; a program needn't handle non-finite values.
Results may differ from a plain program's by a relative error of at most 0.035.
Values may be sent and summed in bfloat16 or wider, within the bound.
No kernel may reach another device: no remote copies, remote signals or barrier semaphores. Data moves between devices by JAX's collectives and lax.ppermute only.
A program may use at most 128 MiB of HBM per device.

v0:
```python
import jax
import jax.numpy as jnp
from jax import lax
from jax.sharding import PartitionSpec as P

HEADS = 16
HEAD_DIM = 128
epsilon_value = 1e-05


def from_behind(shard, axis, by):
    devices = lax.axis_size(axis)
    pairs = [(i, i + by) for i in range(devices) if 0 <= i + by < devices]
    return lax.ppermute(shard, axis, pairs)


def normalize(hidden, gain):
    widened = hidden.astype(jnp.float32)
    mean_square = jnp.mean(widened * widened, axis=-1, keepdims=True)
    return (widened * lax.rsqrt(mean_square + epsilon_value) * gain).astype(jnp.bfloat16)


def head_norm(block, gain, seq_len):
    split = block.reshape(seq_len, HEADS, HEAD_DIM)
    mean_square = jnp.mean(split * split, axis=-1, keepdims=True)
    return (split * lax.rsqrt(mean_square + epsilon_value) * gain.reshape(HEADS, HEAD_DIM)).astype(
        jnp.bfloat16
    )


def finish(hidden, projected, gain_query, gain_key, out_weight, start, length):
    seq_len, model_width = hidden.shape
    queries = head_norm(projected[:, :model_width], gain_query, seq_len)
    key_rows = head_norm(projected[:, model_width : 2 * model_width], gain_key, seq_len)
    value_rows = (
        projected[:, 2 * model_width :].astype(jnp.bfloat16).reshape(seq_len, HEADS, HEAD_DIM)
    )
    scores = jnp.einsum(
        "qhd,khd->hqk", queries, key_rows, preferred_element_type=jnp.float32
    ) * HEAD_DIM ** (-0.5)
    position = jnp.arange(seq_len, dtype=jnp.int32)
    in_image = (position >= start) & (position < start + length)
    allowed = (position[None, :] <= position[:, None]) | in_image[:, None] & in_image[None, :]
    scores = jnp.where(allowed[None], scores, -1e30)
    row_max = jnp.max(scores, axis=-1, keepdims=True)
    lifted = jnp.exp(scores - row_max)
    probabilities = (lifted / jnp.sum(lifted, axis=-1, keepdims=True)).astype(jnp.bfloat16)
    mixed = jnp.einsum(
        "hqk,khd->qhd", probabilities, value_rows, preferred_element_type=jnp.float32
    )
    attended = mixed.reshape(seq_len, model_width).astype(jnp.bfloat16)
    output_rows = jnp.dot(attended, out_weight, preferred_element_type=jnp.float32)
    return (hidden.astype(jnp.float32) + output_rows).astype(jnp.bfloat16)


def body(inputs, order, image_start, image_len, norm_gain, qkv_weight, q_gain, k_gain, o_weight):
    section_count = lax.axis_size("section")
    section_index = lax.axis_index("section")
    micro_count = order.shape[1]
    row_count, model_width = inputs.shape
    seq_len = row_count // micro_count
    ordered = jnp.take(inputs.reshape(micro_count, seq_len, model_width), order[0], axis=0)
    starts = jnp.take(image_start[0], order[0])
    lengths = jnp.take(image_len[0], order[0])
    gain = norm_gain[0]
    gain_query = q_gain[0]
    gain_key = k_gain[0]
    out_weight = o_weight[0]
    shard = qkv_weight[0]
    turns = micro_count + section_count - 1

    def entering(turn_index, incoming):
        fresh = lax.dynamic_index_in_dim(
            ordered, jnp.clip(turn_index, 0, micro_count - 1), 0, keepdims=False
        )
        return jnp.where(section_index == 0, fresh, incoming)

    def settle(turn_index, hidden, project_rows, outputs):
        slot_index = turn_index - section_index
        active = (slot_index >= 0) & (slot_index < micro_count)
        chosen = jnp.clip(slot_index, 0, micro_count - 1)

        def compute(state):
            return finish(
                state,
                project_rows(state),
                gain_query,
                gain_key,
                out_weight,
                starts[chosen],
                lengths[chosen],
            )

        result = lax.cond(active, compute, lambda state: state, hidden)
        outputs = jnp.where(
            active, lax.dynamic_update_index_in_dim(outputs, result, chosen, 0), outputs
        )
        incoming = from_behind(result, "section", 1)
        return (incoming, outputs)

    outputs = jnp.zeros((micro_count, seq_len, model_width), jnp.bfloat16)
    incoming = jnp.zeros((seq_len, model_width), jnp.bfloat16)
    gathered = lax.all_gather(shard, "dp", axis=0, tiled=True)
    first_turn = 0

    def project(state):
        return jnp.dot(normalize(state, gain), gathered, preferred_element_type=jnp.float32)

    def advance(turn_index, carry):
        arriving, collected = carry
        hidden_now = entering(turn_index, arriving)
        return settle(turn_index, hidden_now, project, collected)

    incoming, outputs = lax.fori_loop(first_turn, turns, advance, (incoming, outputs))
    return outputs.reshape(1, row_count, model_width)


def solution(mesh):
    in_specs = (
        P("dp", None),
        P("dp", None),
        P("dp", None),
        P("dp", None),
        P("section", None),
        P("section", "dp", None),
        P("section", None),
        P("section", None),
        P("section", None, None),
    )
    out_specs = P("section", "dp", None)
    return jax.shard_map(body, mesh=mesh, in_specs=in_specs, out_specs=out_specs, check_vma=False)
```

profile of v0, /device:TPU:224, one launch (start us, length us, event | category | flops | bytes accessed | tf_op | source)
XLA Modules:
  0.0 543.5 jit_solution(1400201827899361241)
XLA Ops:
  7.9 1.3 gather_fusion.2
  9.2 1.3 gather_fusion.1
  12.5 1.1 broadcast_select_fusion
  13.6 93.9 %all-gather.3.cloned.1.call-done = bf16[1,2048,6144]{2,1,0:T(8,128)(2,1)} async-done(((bf16[1,64,6144]{2,1,0:T(8,128)(2,1)}), bf16[1,2048,6144]{2,1,0:T(8,128)(2,1)}) %all-gather.3.cloned.1.call-update) | async-done | bytes 25165840 | tf_op jit(solution)/shard_map/all_gather | solution.py:103
  107.6 1.1 broadcast_in_dim.57
  108.6 428.0 %while.16 = (s32[]{:T(128)}, bf16[128,2048]{1,0:T(8,128)(2,1)S(1)}, bf16[2,128,2048]{2,1,0:T(8,128)(2,1)}, s32[]{:T(128)}, pred[]{:T(512)}, /*index=5*/bf16[2,12...) while((s32[]{:T(128)}, bf16[128,2048]{1,0:T(8,128)(2,1)S(1)}, ...), condition=%wide.region_8.10_spmd, body=%wide.region_0.9_spmd.sunk | while | flops 4437105152 | bytes 82586920 | solution.py:114
  108.6 1.1 bitcast_select_fusion.3
  109.8 1.3 collective-permute-start
  111.1 2.0 fusion.27
  113.0 12.7 %collective-permute-done = bf16[128,2048]{1,0:T(8,128)(2,1)S(1)} collective-permute-done((bf16[128,2048]{1,0:T(8,128)(2,1)S(1)}, bf16[128,2048]{1,0:T(8,128)(2,1)S(1)}, u32[]{:S(2)}, u32[]{:S(2)}) %collective-permute-start) | collective-permute-done | bytes 524320 | tf_op jit(solution)/shard_map/while/body/eval_jaxpr/ppermute | solution.py:14
  125.7 1.1 bitcast_select_fusion.3
  126.9 1.3 collective-permute-start
  128.2 2.0 fusion.27
  130.1 11.9 %collective-permute-done = bf16[128,2048]{1,0:T(8,128)(2,1)S(1)} collective-permute-done((bf16[128,2048]{1,0:T(8,128)(2,1)S(1)}, bf16[128,2048]{1,0:T(8,128)(2,1)S(1)}, u32[]{:S(2)}, u32[]{:S(2)}) %collective-permute-start) | collective-permute-done | bytes 524320 | tf_op jit(solution)/shard_map/while/body/eval_jaxpr/ppermute | solution.py:14
  142.0 1.1 bitcast_select_fusion.3
  143.2 1.3 collective-permute-start
  144.5 2.0 fusion.27
  146.4 11.0 %collective-permute-done = bf16[128,2048]{1,0:T(8,128)(2,1)S(1)} collective-permute-done((bf16[128,2048]{1,0:T(8,128)(2,1)S(1)}, bf16[128,2048]{1,0:T(8,128)(2,1)S(1)}, u32[]{:S(2)}, u32[]{:S(2)}) %collective-permute-start) | collective-permute-done | bytes 524320 | tf_op jit(solution)/shard_map/while/body/eval_jaxpr/ppermute | solution.py:14
  157.4 1.1 bitcast_select_fusion.3
  158.5 1.3 collective-permute-start
  159.8 2.0 fusion.27
  161.8 11.1 %collective-permute-done = bf16[128,2048]{1,0:T(8,128)(2,1)S(1)} collective-permute-done((bf16[128,2048]{1,0:T(8,128)(2,1)S(1)}, bf16[128,2048]{1,0:T(8,128)(2,1)S(1)}, u32[]{:S(2)}, u32[]{:S(2)}) %collective-permute-start) | collective-permute-done | bytes 524320 | tf_op jit(solution)/shard_map/while/body/eval_jaxpr/ppermute | solution.py:14
  172.9 1.1 bitcast_select_fusion.3
  174.0 1.3 collective-permute-start
  175.3 2.0 fusion.27
  177.3 10.3 %collective-permute-done = bf16[128,2048]{1,0:T(8,128)(2,1)S(1)} collective-permute-done((bf16[128,2048]{1,0:T(8,128)(2,1)S(1)}, bf16[128,2048]{1,0:T(8,128)(2,1)S(1)}, u32[]{:S(2)}, u32[]{:S(2)}) %collective-permute-start) | collective-permute-done | bytes 524320 | tf_op jit(solution)/shard_map/while/body/eval_jaxpr/ppermute | solution.py:14
  187.5 1.1 bitcast_select_fusion.3
  188.7 1.3 collective-permute-start
  190.0 2.0 fusion.27
  191.9 9.4 %collective-permute-done = bf16[128,2048]{1,0:T(8,128)(2,1)S(1)} collective-permute-done((bf16[128,2048]{1,0:T(8,128)(2,1)S(1)}, bf16[128,2048]{1,0:T(8,128)(2,1)S(1)}, u32[]{:S(2)}, u32[]{:S(2)}) %collective-permute-start) | collective-permute-done | bytes 524320 | tf_op jit(solution)/shard_map/while/body/eval_jaxpr/ppermute | solution.py:14
  201.3 1.1 bitcast_select_fusion.3
  202.5 1.3 collective-permute-start
  203.8 2.0 fusion.27
  205.7 238.5 %collective-permute-done = bf16[128,2048]{1,0:T(8,128)(2,1)S(1)} collective-permute-done((bf16[128,2048]{1,0:T(8,128)(2,1)S(1)}, bf16[128,2048]{1,0:T(8,128)(2,1)S(1)}, u32[]{:S(2)}, u32[]{:S(2)}) %collective-permute-start) | collective-permute-done | bytes 524320 | tf_op jit(solution)/shard_map/while/body/eval_jaxpr/ppermute | solution.py:14
  444.2 1.1 bitcast_select_fusion.3
  445.3 33.6 %conditional.2 = (bf16[128,2048]{1,0:T(8,128)(2,1)S(1)}) conditional(s32[]{:T(128)} %convert_element_type.56, bf16[128,2048]{1,0:T(8,128)(2,1)S(1)} %bitcast_select_fusion.3, (bf16[128,2048]{1,0:T(8,128)(2,1)S(1)}, f32[1,2048]{1,0:T(1,128)}, bf16[2048,6144]{1,0:T(8,128)(2,1)}, s32[]{:T(128)}, s32[2]{0:T(128)S(1)}, /*index=5*/s32[2]{0:T(128)S(1)}, ...), branch_computations={%region_1.2_spmd, %region_2.8_spmd} | conditional | flops 4436580864 | bytes 77343176 | solution.py:94
  445.5 10.1 %fusion.8 = f32[128,6144]{1,0:T(8,128)S(1)} fusion(bf16[2048,6144]{1,0:T(8,128)(2,1)} %get-tuple-element.278, bf16[128,2048]{1,0:T(8,128)(2,1)S(1)} %get-tuple-element.276, f32[2048]{0:T(1024)} %bitcast.57, f32[128]{0:T(128)S(1)} %add_rsqrt_fusion.2), kind=kOutput, calls=%fused_computation.24 | convolution fusion | flops 3222274048 | bytes 28844544 | tf_op jit(solution)/shard_map/while/body/eval_jaxpr/cond/branch_1_fun/dot_general | solution.py:107
  455.7 1.7 copy-done.1
  457.5 1.0 copy.31
  458.5 2.8 slice_bitcast_fusion.1
  462.0 1.4 copy.32
  463.4 1.1 copy-done.2
  465.0 2.7 multiply_convert_fusion
  470.8 1.7 fusion.4
  472.7 1.5 convolution_convert_fusion
  474.2 4.7 fusion.1
  478.9 1.3 collective-permute-start
  480.2 2.0 fusion.27
  482.1 8.8 %collective-permute-done = bf16[128,2048]{1,0:T(8,128)(2,1)S(1)} collective-permute-done((bf16[128,2048]{1,0:T(8,128)(2,1)S(1)}, bf16[128,2048]{1,0:T(8,128)(2,1)S(1)}, u32[]{:S(2)}, u32[]{:S(2)}) %collective-permute-start) | collective-permute-done | bytes 524320 | tf_op jit(solution)/shard_map/while/body/eval_jaxpr/ppermute | solution.py:14
  491.0 1.1 bitcast_select_fusion.3
  492.1 33.6 %conditional.2 = (bf16[128,2048]{1,0:T(8,128)(2,1)S(1)}) conditional(s32[]{:T(128)} %convert_element_type.56, bf16[128,2048]{1,0:T(8,128)(2,1)S(1)} %bitcast_select_fusion.3, (bf16[128,2048]{1,0:T(8,128)(2,1)S(1)}, f32[1,2048]{1,0:T(1,128)}, bf16[2048,6144]{1,0:T(8,128)(2,1)}, s32[]{:T(128)}, s32[2]{0:T(128)S(1)}, /*index=5*/s32[2]{0:T(128)S(1)}, ...), branch_computations={%region_1.2_spmd, %region_2.8_spmd} | conditional | flops 4436580864 | bytes 77343176 | solution.py:94
  492.3 10.1 %fusion.8 = f32[128,6144]{1,0:T(8,128)S(1)} fusion(bf16[2048,6144]{1,0:T(8,128)(2,1)} %get-tuple-element.278, bf16[128,2048]{1,0:T(8,128)(2,1)S(1)} %get-tuple-element.276, f32[2048]{0:T(1024)} %bitcast.57, f32[128]{0:T(128)S(1)} %add_rsqrt_fusion.2), kind=kOutput, calls=%fused_computation.24 | convolution fusion | flops 3222274048 | bytes 28844544 | tf_op jit(solution)/shard_map/while/body/eval_jaxpr/cond/branch_1_fun/dot_general | solution.py:107
  502.4 1.7 copy-done.1
  504.2 1.0 copy.31
  505.2 2.8 slice_bitcast_fusion.1
  508.7 1.4 copy.32
  510.1 1.1 copy-done.2
  511.8 2.7 multiply_convert_fusion
  517.5 1.7 fusion.4
  519.4 1.5 convolution_convert_fusion
  520.9 4.7 fusion.1
  525.6 1.3 collective-permute-start
  526.9 2.0 fusion.27
  528.9 7.8 %collective-permute-done = bf16[128,2048]{1,0:T(8,128)(2,1)S(1)} collective-permute-done((bf16[128,2048]{1,0:T(8,128)(2,1)S(1)}, bf16[128,2048]{1,0:T(8,128)(2,1)S(1)}, u32[]{:S(2)}, u32[]{:S(2)}) %collective-permute-start) | collective-permute-done | bytes 524320 | tf_op jit(solution)/shard_map/while/body/eval_jaxpr/ppermute | solution.py:14
  (65 shorter events, 10.6 us)
Async XLA Ops:
  6.5 4.7 copy-start
  6.5 101.0 %all-gather.3.cloned.1.call-start = ((), (), s32[]{:S(2)}) async-start(), calls=%async_computation | async-start | bytes 25952256 | tf_op jit(solution)/shard_map/all_gather | solution.py:103
  109.8 16.0 %collective-permute-start = (bf16[128,2048]{1,0:T(8,128)(2,1)S(1)}, bf16[128,2048]{1,0:T(8,128)(2,1)S(1)}, u32[]{:S(2)}, u32[]{:S(2)}) collective-permute-start(bf16[128,2048]{1,0:T(8,128)(2,1)S(1)} %get-tuple-element.460), channel_id=1, source_target_pairs={{0,32},{32,64},{64,96},{96,128},{128,160},{160,192},{192,224},{1,3... | collective-permute-start | bytes 1572872 | tf_op jit(solution)/shard_map/while/body/eval_jaxpr/ppermute | solution.py:14
  126.9 15.2 %collective-permute-start = (bf16[128,2048]{1,0:T(8,128)(2,1)S(1)}, bf16[128,2048]{1,0:T(8,128)(2,1)S(1)}, u32[]{:S(2)}, u32[]{:S(2)}) collective-permute-start(bf16[128,2048]{1,0:T(8,128)(2,1)S(1)} %get-tuple-element.460), channel_id=1, source_target_pairs={{0,32},{32,64},{64,96},{96,128},{128,160},{160,192},{192,224},{1,3... | collective-permute-start | bytes 1572872 | tf_op jit(solution)/shard_map/while/body/eval_jaxpr/ppermute | solution.py:14
  143.2 14.2 %collective-permute-start = (bf16[128,2048]{1,0:T(8,128)(2,1)S(1)}, bf16[128,2048]{1,0:T(8,128)(2,1)S(1)}, u32[]{:S(2)}, u32[]{:S(2)}) collective-permute-start(bf16[128,2048]{1,0:T(8,128)(2,1)S(1)} %get-tuple-element.460), channel_id=1, source_target_pairs={{0,32},{32,64},{64,96},{96,128},{128,160},{160,192},{192,224},{1,3... | collective-permute-start | bytes 1572872 | tf_op jit(solution)/shard_map/while/body/eval_jaxpr/ppermute | solution.py:14
  158.5 14.4 %collective-permute-start = (bf16[128,2048]{1,0:T(8,128)(2,1)S(1)}, bf16[128,2048]{1,0:T(8,128)(2,1)S(1)}, u32[]{:S(2)}, u32[]{:S(2)}) collective-permute-start(bf16[128,2048]{1,0:T(8,128)(2,1)S(1)} %get-tuple-element.460), channel_id=1, source_target_pairs={{0,32},{32,64},{64,96},{96,128},{128,160},{160,192},{192,224},{1,3... | collective-permute-start | bytes 1572872 | tf_op jit(solution)/shard_map/while/body/eval_jaxpr/ppermute | solution.py:14
  174.0 13.5 %collective-permute-start = (bf16[128,2048]{1,0:T(8,128)(2,1)S(1)}, bf16[128,2048]{1,0:T(8,128)(2,1)S(1)}, u32[]{:S(2)}, u32[]{:S(2)}) collective-permute-start(bf16[128,2048]{1,0:T(8,128)(2,1)S(1)} %get-tuple-element.460), channel_id=1, source_target_pairs={{0,32},{32,64},{64,96},{96,128},{128,160},{160,192},{192,224},{1,3... | collective-permute-start | bytes 1572872 | tf_op jit(solution)/shard_map/while/body/eval_jaxpr/ppermute | solution.py:14
  188.7 12.7 %collective-permute-start = (bf16[128,2048]{1,0:T(8,128)(2,1)S(1)}, bf16[128,2048]{1,0:T(8,128)(2,1)S(1)}, u32[]{:S(2)}, u32[]{:S(2)}) collective-permute-start(bf16[128,2048]{1,0:T(8,128)(2,1)S(1)} %get-tuple-element.460), channel_id=1, source_target_pairs={{0,32},{32,64},{64,96},{96,128},{128,160},{160,192},{192,224},{1,3... | collective-permute-start | bytes 1572872 | tf_op jit(solution)/shard_map/while/body/eval_jaxpr/ppermute | solution.py:14
  202.5 241.7 %collective-permute-start = (bf16[128,2048]{1,0:T(8,128)(2,1)S(1)}, bf16[128,2048]{1,0:T(8,128)(2,1)S(1)}, u32[]{:S(2)}, u32[]{:S(2)}) collective-permute-start(bf16[128,2048]{1,0:T(8,128)(2,1)S(1)} %get-tuple-element.460), channel_id=1, source_target_pairs={{0,32},{32,64},{64,96},{96,128},{128,160},{160,192},{192,224},{1,3... | collective-permute-start | bytes 1572872 | tf_op jit(solution)/shard_map/while/body/eval_jaxpr/ppermute | solution.py:14
  455.6 1.8 copy-start.1
  457.4 7.6 %copy-start.3 = (f32[1,2048]{1,0:T(1,128)S(1)}, f32[1,2048]{1,0:T(1,128)}, u32[]{:S(2)}) copy-start(f32[1,2048]{1,0:T(1,128)} %get-tuple-element.282) | copy-start | bytes 24580 | tf_op jit(solution)/shard_map/while/body/eval_jaxpr/cond
  457.4 7.6 %copy-start.4 = (f32[1,2048]{1,0:T(1,128)S(1)}, f32[1,2048]{1,0:T(1,128)}, u32[]{:S(2)}) copy-start(f32[1,2048]{1,0:T(1,128)} %get-tuple-element.283) | copy-start | bytes 24580 | tf_op jit(solution)/shard_map/while/body/eval_jaxpr/cond
  463.4 1.1 copy-start.2
  478.9 12.1 %collective-permute-start = (bf16[128,2048]{1,0:T(8,128)(2,1)S(1)}, bf16[128,2048]{1,0:T(8,128)(2,1)S(1)}, u32[]{:S(2)}, u32[]{:S(2)}) collective-permute-start(bf16[128,2048]{1,0:T(8,128)(2,1)S(1)} %get-tuple-element.460), channel_id=1, source_target_pairs={{0,32},{32,64},{64,96},{96,128},{128,160},{160,192},{192,224},{1,3... | collective-permute-start | bytes 1572872 | tf_op jit(solution)/shard_map/while/body/eval_jaxpr/ppermute | solution.py:14
  502.4 1.8 copy-start.1
  504.2 7.6 %copy-start.3 = (f32[1,2048]{1,0:T(1,128)S(1)}, f32[1,2048]{1,0:T(1,128)}, u32[]{:S(2)}) copy-start(f32[1,2048]{1,0:T(1,128)} %get-tuple-element.282) | copy-start | bytes 24580 | tf_op jit(solution)/shard_map/while/body/eval_jaxpr/cond
  504.2 7.6 %copy-start.4 = (f32[1,2048]{1,0:T(1,128)S(1)}, f32[1,2048]{1,0:T(1,128)}, u32[]{:S(2)}) copy-start(f32[1,2048]{1,0:T(1,128)} %get-tuple-element.283) | copy-start | bytes 24580 | tf_op jit(solution)/shard_map/while/body/eval_jaxpr/cond
  510.1 1.1 copy-start.2
  525.6 11.1 %collective-permute-start = (bf16[128,2048]{1,0:T(8,128)(2,1)S(1)}, bf16[128,2048]{1,0:T(8,128)(2,1)S(1)}, u32[]{:S(2)}, u32[]{:S(2)}) collective-permute-start(bf16[128,2048]{1,0:T(8,128)(2,1)S(1)} %get-tuple-element.460), channel_id=1, source_target_pairs={{0,32},{32,64},{64,96},{96,128},{128,160},{160,192},{192,224},{1,3... | collective-permute-start | bytes 1572872 | tf_op jit(solution)/shard_map/while/body/eval_jaxpr/ppermute | solution.py:14
Sparse Core Ops, SparseCore 0:
  9.9 97.5 all-gather.2
where the time goes:
time: 545 us; the launch traced here: 544 us
  waiting for transfers between devices  416 us (76%)
  other arithmetic  39.8 us (7%)
  matrix products  35.9 us (7%)
  local copies, waits for them, and re-layouts  23.8 us (4%)
  between operations  13.4 us (2%)
  starting transfers between devices  11.6 us (2%)
    ppermute x9, waiting for transfers between devices, from_behind(): return lax.ppermute(shard, axis, pairs)  321 us
    all_gather x1, waiting for transfers between devices, body(): gathered = lax.all_gather(shard, 'dp', axis=0, tiled=True)  93.9 us
    dot_general x2, matrix products, project(): jnp.dot(normalize(state, gain), gathered, preferred_element_type=jnp.floa...  20.3 us
    select_n x9, other arithmetic, settle(): jnp.where(active, lax.dynamic_update_index_in_dim(outputs, result, chosen...  17.7 us
    cond x22, local copies, waits for them, and re-layouts  14.4 us
    ppermute x9, starting transfers between devices, from_behind(): return lax.ppermute(shard, axis, pairs)  11.6 us
  transfers between devices with their start and end apart: 10, of which 10 were waited for; matrix products, arithmetic and copies ran while one was open for 4% of the time, Pallas kernels for 0%

commit v1 on v0

--- a/solution.py
+++ b/solution.py
@@ -100,7 +100,9 @@
 
     outputs = jnp.zeros((micro_count, seq_len, model_width), jnp.bfloat16)
     incoming = jnp.zeros((seq_len, model_width), jnp.bfloat16)
-    gathered = lax.all_gather(shard, "dp", axis=0, tiled=True)
+    gathered = jnp.concatenate(
+        lax.all_to_all(jnp.stack([shard] * lax.axis_size("dp")), "dp", 0, 0), axis=0
+    )
     first_turn = 0
 
     def project(state):

time: 545 us -> 814 us (1.49)
  the two profiles are of different devices: /device:TPU:224 before, /device:TPU:236 now
where the time goes in v1:
time: 814 us; the launch traced here: 812 us
  waiting for transfers between devices  691 us (85%)
  other arithmetic  35.7 us (4%)
  matrix products  33.5 us (4%)
  local copies, waits for them, and re-layouts  29.2 us (4%)
  starting transfers between devices  19.3 us (2%)
    all_to_all x1, waiting for transfers between devices, body(): lax.all_to_all(jnp.stack([shard] * lax.axis_size('dp')), 'dp', 0, 0)  408 us
    ppermute x9, waiting for transfers between devices, from_behind(): return lax.ppermute(shard, axis, pairs)  283 us
    dot_general x2, matrix products, project(): jnp.dot(normalize(state, gain), gathered, preferred_element_type=jnp.floa...  20.2 us
    select_n x9, other arithmetic, settle(): jnp.where(active, lax.dynamic_update_index_in_dim(outputs, result, chosen...  17.7 us
  transfers between devices with their start and end apart: 10, of which 10 were waited for; matrix products, arithmetic and copies ran while one was open for 3% of the time, Pallas kernels for 0%

profile of v1, /device:TPU:236, one launch (start us, length us, event | category | flops | bytes accessed | tf_op | source)
XLA Modules:
  0.0 812.4 jit_solution(17417491392385309636)
XLA Ops:
  0.0 9.6 %stack.3 = bf16[32,64,6144]{2,1,0:T(8,128)(2,1)} broadcast(bf16[64,6144]{1,0:T(8,128)(2,1)} %bitcast.58), dimensions={1,2} | broadcast | bytes 25952256 | tf_op jit(solution)/shard_map/stack | solution.py:104
  9.7 7.7 all-to-all-start
  19.4 1.1 broadcast_select_fusion
  20.5 408.4 %all-to-all-done = bf16[32,64,6144]{2,1,0:T(8,128)(2,1)} async-done(((bf16[32,64,6144]{2,1,0:T(8,128)(2,1)}), bf16[32,64,6144]{2,1,0:T(8,128)(2,1)}, u32[]{:S(2)}, u32[]{:S(2)}) %all-to-all-start) | async-done | bytes 25165856 | tf_op jit(solution)/shard_map/all_to_all | solution.py:104
  428.9 1.1 broadcast_in_dim.57
  430.1 381.1 %while.16 = (s32[]{:T(128)}, bf16[128,2048]{1,0:T(8,128)(2,1)S(1)}, bf16[2,128,2048]{2,1,0:T(8,128)(2,1)}, s32[]{:T(128)}, pred[]{:T(512)}, /*index=5*/bf16[2,12...) while((s32[]{:T(128)}, bf16[128,2048]{1,0:T(8,128)(2,1)S(1)}, ...), condition=%wide.region_8.10_spmd, body=%wide.region_0.9_spmd.sunk | while | flops 4437105152 | bytes 78326992 | solution.py:116
  430.1 1.1 bitcast_select_fusion.3
  431.2 1.3 collective-permute-start
  432.5 2.0 fusion.27
  434.5 12.1 %collective-permute-done = bf16[128,2048]{1,0:T(8,128)(2,1)S(1)} collective-permute-done((bf16[128,2048]{1,0:T(8,128)(2,1)S(1)}, bf16[128,2048]{1,0:T(8,128)(2,1)S(1)}, u32[]{:S(2)}, u32[]{:S(2)}) %collective-permute-start) | collective-permute-done | bytes 524320 | tf_op jit(solution)/shard_map/while/body/eval_jaxpr/ppermute | solution.py:14
  446.6 1.1 bitcast_select_fusion.3
  447.7 1.3 collective-permute-start
  449.0 2.0 fusion.27
  451.0 11.2 %collective-permute-done = bf16[128,2048]{1,0:T(8,128)(2,1)S(1)} collective-permute-done((bf16[128,2048]{1,0:T(8,128)(2,1)S(1)}, bf16[128,2048]{1,0:T(8,128)(2,1)S(1)}, u32[]{:S(2)}, u32[]{:S(2)}) %collective-permute-start) | collective-permute-done | bytes 524320 | tf_op jit(solution)/shard_map/while/body/eval_jaxpr/ppermute | solution.py:14
  462.2 1.1 bitcast_select_fusion.3
  463.3 1.3 collective-permute-start
  464.6 2.0 fusion.27
  466.5 10.3 %collective-permute-done = bf16[128,2048]{1,0:T(8,128)(2,1)S(1)} collective-permute-done((bf16[128,2048]{1,0:T(8,128)(2,1)S(1)}, bf16[128,2048]{1,0:T(8,128)(2,1)S(1)}, u32[]{:S(2)}, u32[]{:S(2)}) %collective-permute-start) | collective-permute-done | bytes 524320 | tf_op jit(solution)/shard_map/while/body/eval_jaxpr/ppermute | solution.py:14
  476.8 1.1 bitcast_select_fusion.3
  477.9 1.3 collective-permute-start
  479.2 2.0 fusion.27
  481.2 9.3 %collective-permute-done = bf16[128,2048]{1,0:T(8,128)(2,1)S(1)} collective-permute-done((bf16[128,2048]{1,0:T(8,128)(2,1)S(1)}, bf16[128,2048]{1,0:T(8,128)(2,1)S(1)}, u32[]{:S(2)}, u32[]{:S(2)}) %collective-permute-start) | collective-permute-done | bytes 524320 | tf_op jit(solution)/shard_map/while/body/eval_jaxpr/ppermute | solution.py:14
  490.5 1.1 bitcast_select_fusion.3
  491.7 1.3 collective-permute-start
  493.0 2.0 fusion.27
  494.9 9.5 %collective-permute-done = bf16[128,2048]{1,0:T(8,128)(2,1)S(1)} collective-permute-done((bf16[128,2048]{1,0:T(8,128)(2,1)S(1)}, bf16[128,2048]{1,0:T(8,128)(2,1)S(1)}, u32[]{:S(2)}, u32[]{:S(2)}) %collective-permute-start) | collective-permute-done | bytes 524320 | tf_op jit(solution)/shard_map/while/body/eval_jaxpr/ppermute | solution.py:14
  504.4 1.1 bitcast_select_fusion.3
  505.6 1.3 collective-permute-start
  506.9 2.0 fusion.27
  508.8 8.7 %collective-permute-done = bf16[128,2048]{1,0:T(8,128)(2,1)S(1)} collective-permute-done((bf16[128,2048]{1,0:T(8,128)(2,1)S(1)}, bf16[128,2048]{1,0:T(8,128)(2,1)S(1)}, u32[]{:S(2)}, u32[]{:S(2)}) %collective-permute-start) | collective-permute-done | bytes 524320 | tf_op jit(solution)/shard_map/while/body/eval_jaxpr/ppermute | solution.py:14
  517.5 1.1 bitcast_select_fusion.3
  518.7 1.3 collective-permute-start
  520.0 2.0 fusion.27
  521.9 206.0 %collective-permute-done = bf16[128,2048]{1,0:T(8,128)(2,1)S(1)} collective-permute-done((bf16[128,2048]{1,0:T(8,128)(2,1)S(1)}, bf16[128,2048]{1,0:T(8,128)(2,1)S(1)}, u32[]{:S(2)}, u32[]{:S(2)}) %collective-permute-start) | collective-permute-done | bytes 524320 | tf_op jit(solution)/shard_map/while/body/eval_jaxpr/ppermute | solution.py:14
  727.9 1.1 bitcast_select_fusion.3
  729.0 29.3 %conditional.2 = (bf16[128,2048]{1,0:T(8,128)(2,1)S(1)}) conditional(s32[]{:T(128)} %convert_element_type.56, bf16[128,2048]{1,0:T(8,128)(2,1)S(1)} %bitcast_select_fusion.3, (bf16[128,2048]{1,0:T(8,128)(2,1)S(1)}, f32[1,2048]{1,0:T(1,128)S(1)}, bf16[2048,6144]{1,0:T(8,128)(2,1)}, s32[]{:T(128)}, s32[2]{0:T(128)S(1)}, /*index=5*/s32[2]{0:T(128)S(1)}, ...), branch_computations={%region_1.2_spmd, %region_2.8_spmd} | conditional | flops 4436580864 | bytes 73083248 | solution.py:94
  729.2 10.1 %fusion.8 = f32[128,6144]{1,0:T(8,128)S(1)} fusion(bf16[2048,6144]{1,0:T(8,128)(2,1)} %get-tuple-element.278, bf16[128,2048]{1,0:T(8,128)(2,1)S(1)} %get-tuple-element.276, f32[2048]{0:T(1024)S(1)} %bitcast.57, f32[128]{0:T(128)S(1)} %add_rsqrt_fusion.2), kind=kOutput, calls=%fused_computation.24 | convolution fusion | flops 3222274048 | bytes 28844544 | tf_op jit(solution)/shard_map/while/body/eval_jaxpr/cond/branch_1_fun/dot_general | solution.py:109
  739.3 1.8 copy-done.4
  741.1 1.1 slice_bitcast_fusion.1
  742.9 1.4 copy.33
  744.9 1.6 multiply_convert_fusion
  746.5 0.7 dynamic_slice.12
  749.0 0.7 compare_and_fusion
  749.8 1.5 fusion.4
  751.6 1.3 slice.22
  753.6 4.7 fusion.1
  758.3 1.3 collective-permute-start
  759.6 2.0 fusion.27
  761.6 8.2 %collective-permute-done = bf16[128,2048]{1,0:T(8,128)(2,1)S(1)} collective-permute-done((bf16[128,2048]{1,0:T(8,128)(2,1)S(1)}, bf16[128,2048]{1,0:T(8,128)(2,1)S(1)}, u32[]{:S(2)}, u32[]{:S(2)}) %collective-permute-start) | collective-permute-done | bytes 524320 | tf_op jit(solution)/shard_map/while/body/eval_jaxpr/ppermute | solution.py:14
  769.7 1.1 bitcast_select_fusion.3
  770.8 29.3 %conditional.2 = (bf16[128,2048]{1,0:T(8,128)(2,1)S(1)}) conditional(s32[]{:T(128)} %convert_element_type.56, bf16[128,2048]{1,0:T(8,128)(2,1)S(1)} %bitcast_select_fusion.3, (bf16[128,2048]{1,0:T(8,128)(2,1)S(1)}, f32[1,2048]{1,0:T(1,128)S(1)}, bf16[2048,6144]{1,0:T(8,128)(2,1)}, s32[]{:T(128)}, s32[2]{0:T(128)S(1)}, /*index=5*/s32[2]{0:T(128)S(1)}, ...), branch_computations={%region_1.2_spmd, %region_2.8_spmd} | conditional | flops 4436580864 | bytes 73083248 | solution.py:94
  771.0 10.1 %fusion.8 = f32[128,6144]{1,0:T(8,128)S(1)} fusion(bf16[2048,6144]{1,0:T(8,128)(2,1)} %get-tuple-element.278, bf16[128,2048]{1,0:T(8,128)(2,1)S(1)} %get-tuple-element.276, f32[2048]{0:T(1024)S(1)} %bitcast.57, f32[128]{0:T(128)S(1)} %add_rsqrt_fusion.2), kind=kOutput, calls=%fused_computation.24 | convolution fusion | flops 3222274048 | bytes 28844544 | tf_op jit(solution)/shard_map/while/body/eval_jaxpr/cond/branch_1_fun/dot_general | solution.py:109
  781.2 1.8 copy-done.4
  782.9 1.1 slice_bitcast_fusion.1
  784.8 1.4 copy.33
  786.7 1.6 multiply_convert_fusion
  790.9 0.7 compare_and_fusion
  791.7 1.5 fusion.4
  793.4 1.3 slice.22
  795.4 4.7 fusion.1
  800.1 1.3 collective-permute-start
  801.4 2.0 fusion.27
  803.4 7.8 collective-permute-done
  811.2 1.2 copy-done.1
  (67 shorter events, 8.8 us)
Async XLA Ops:
  0.0 18.7 %copy-start = (bf16[256,2048]{1,0:T(8,128)(2,1)S(1)}, bf16[256,2048]{1,0:T(8,128)(2,1)}, u32[]{:S(2)}) copy-start(bf16[256,2048]{1,0:T(8,128)(2,1)} %param.15) | copy-start | bytes 3145732
  9.6 7.7 copy-start.8
  9.6 7.8 copy-start.2
  9.6 8.4 %copy-start.3 = (s32[1,2]{1,0:T(1,128)S(1)}, s32[1,2]{1,0:T(1,128)}, u32[]{:S(2)}) copy-start(s32[1,2]{1,0:T(1,128)} %param.17) | copy-start | bytes 28
  9.6 420.4 %copy-start.5 = (f32[1,2048]{1,0:T(1,128)S(1)}, f32[1,2048]{1,0:T(1,128)}, u32[]{:S(2)}) copy-start(f32[1,2048]{1,0:T(1,128)} %param.19) | copy-start | bytes 24580
  9.6 420.4 %copy-start.6 = (f32[1,2048]{1,0:T(1,128)S(1)}, f32[1,2048]{1,0:T(1,128)}, u32[]{:S(2)}) copy-start(f32[1,2048]{1,0:T(1,128)} %param.21) | copy-start | bytes 24580
  9.7 420.4 %copy-start.7 = (f32[1,2048]{1,0:T(1,128)S(1)}, f32[1,2048]{1,0:T(1,128)}, u32[]{:S(2)}) copy-start(f32[1,2048]{1,0:T(1,128)} %param.22) | copy-start | bytes 24580
  9.7 419.2 %all-to-all-start = ((bf16[32,64,6144]{2,1,0:T(8,128)(2,1)}), bf16[32,64,6144]{2,1,0:T(8,128)(2,1)}, u32[]{:S(2)}, u32[]{:S(2)}) async-start(bf16[32,64,6144]{2,1,0:T(8,128)(2,1)} %stack.3), calls=%async_computation | async-start | bytes 50331648 | tf_op jit(solution)/shard_map/all_to_all | solution.py:104
  431.2 15.4 %collective-permute-start = (bf16[128,2048]{1,0:T(8,128)(2,1)S(1)}, bf16[128,2048]{1,0:T(8,128)(2,1)S(1)}, u32[]{:S(2)}, u32[]{:S(2)}) collective-permute-start(bf16[128,2048]{1,0:T(8,128)(2,1)S(1)} %get-tuple-element.460), channel_id=1, source_target_pairs={{0,32},{32,64},{64,96},{96,128},{128,160},{160,192},{192,224},{1,3... | collective-permute-start | bytes 1572872 | tf_op jit(solution)/shard_map/while/body/eval_jaxpr/ppermute | solution.py:14
  447.7 14.5 %collective-permute-start = (bf16[128,2048]{1,0:T(8,128)(2,1)S(1)}, bf16[128,2048]{1,0:T(8,128)(2,1)S(1)}, u32[]{:S(2)}, u32[]{:S(2)}) collective-permute-start(bf16[128,2048]{1,0:T(8,128)(2,1)S(1)} %get-tuple-element.460), channel_id=1, source_target_pairs={{0,32},{32,64},{64,96},{96,128},{128,160},{160,192},{192,224},{1,3... | collective-permute-start | bytes 1572872 | tf_op jit(solution)/shard_map/while/body/eval_jaxpr/ppermute | solution.py:14
  463.3 13.5 %collective-permute-start = (bf16[128,2048]{1,0:T(8,128)(2,1)S(1)}, bf16[128,2048]{1,0:T(8,128)(2,1)S(1)}, u32[]{:S(2)}, u32[]{:S(2)}) collective-permute-start(bf16[128,2048]{1,0:T(8,128)(2,1)S(1)} %get-tuple-element.460), channel_id=1, source_target_pairs={{0,32},{32,64},{64,96},{96,128},{128,160},{160,192},{192,224},{1,3... | collective-permute-start | bytes 1572872 | tf_op jit(solution)/shard_map/while/body/eval_jaxpr/ppermute | solution.py:14
  477.9 12.6 %collective-permute-start = (bf16[128,2048]{1,0:T(8,128)(2,1)S(1)}, bf16[128,2048]{1,0:T(8,128)(2,1)S(1)}, u32[]{:S(2)}, u32[]{:S(2)}) collective-permute-start(bf16[128,2048]{1,0:T(8,128)(2,1)S(1)} %get-tuple-element.460), channel_id=1, source_target_pairs={{0,32},{32,64},{64,96},{96,128},{128,160},{160,192},{192,224},{1,3... | collective-permute-start | bytes 1572872 | tf_op jit(solution)/shard_map/while/body/eval_jaxpr/ppermute | solution.py:14
  491.7 12.8 %collective-permute-start = (bf16[128,2048]{1,0:T(8,128)(2,1)S(1)}, bf16[128,2048]{1,0:T(8,128)(2,1)S(1)}, u32[]{:S(2)}, u32[]{:S(2)}) collective-permute-start(bf16[128,2048]{1,0:T(8,128)(2,1)S(1)} %get-tuple-element.460), channel_id=1, source_target_pairs={{0,32},{32,64},{64,96},{96,128},{128,160},{160,192},{192,224},{1,3... | collective-permute-start | bytes 1572872 | tf_op jit(solution)/shard_map/while/body/eval_jaxpr/ppermute | solution.py:14
  505.6 12.0 %collective-permute-start = (bf16[128,2048]{1,0:T(8,128)(2,1)S(1)}, bf16[128,2048]{1,0:T(8,128)(2,1)S(1)}, u32[]{:S(2)}, u32[]{:S(2)}) collective-permute-start(bf16[128,2048]{1,0:T(8,128)(2,1)S(1)} %get-tuple-element.460), channel_id=1, source_target_pairs={{0,32},{32,64},{64,96},{96,128},{128,160},{160,192},{192,224},{1,3... | collective-permute-start | bytes 1572872 | tf_op jit(solution)/shard_map/while/body/eval_jaxpr/ppermute | solution.py:14
  518.7 209.2 %collective-permute-start = (bf16[128,2048]{1,0:T(8,128)(2,1)S(1)}, bf16[128,2048]{1,0:T(8,128)(2,1)S(1)}, u32[]{:S(2)}, u32[]{:S(2)}) collective-permute-start(bf16[128,2048]{1,0:T(8,128)(2,1)S(1)} %get-tuple-element.460), channel_id=1, source_target_pairs={{0,32},{32,64},{64,96},{96,128},{128,160},{160,192},{192,224},{1,3... | collective-permute-start | bytes 1572872 | tf_op jit(solution)/shard_map/while/body/eval_jaxpr/ppermute | solution.py:14
  739.3 1.8 copy-start.4
  758.3 11.4 %collective-permute-start = (bf16[128,2048]{1,0:T(8,128)(2,1)S(1)}, bf16[128,2048]{1,0:T(8,128)(2,1)S(1)}, u32[]{:S(2)}, u32[]{:S(2)}) collective-permute-start(bf16[128,2048]{1,0:T(8,128)(2,1)S(1)} %get-tuple-element.460), channel_id=1, source_target_pairs={{0,32},{32,64},{64,96},{96,128},{128,160},{160,192},{192,224},{1,3... | collective-permute-start | bytes 1572872 | tf_op jit(solution)/shard_map/while/body/eval_jaxpr/ppermute | solution.py:14
  781.2 1.8 copy-start.4
  800.1 11.1 %collective-permute-start = (bf16[128,2048]{1,0:T(8,128)(2,1)S(1)}, bf16[128,2048]{1,0:T(8,128)(2,1)S(1)}, u32[]{:S(2)}, u32[]{:S(2)}) collective-permute-start(bf16[128,2048]{1,0:T(8,128)(2,1)S(1)} %get-tuple-element.460), channel_id=1, source_target_pairs={{0,32},{32,64},{64,96},{96,128},{128,160},{160,192},{192,224},{1,3... | collective-permute-start | bytes 1572872 | tf_op jit(solution)/shard_map/while/body/eval_jaxpr/ppermute | solution.py:14
  811.2 1.2 copy-start.1
